TPU v7x, 32 devices: a whole 2x2x4 slice. The times are simulated.
32 devices in a mesh: dp: 16 (over z, y, x), cls: 2 (over core).
Axes of the slice: x: 2, y: 2, z: 4, core: 2. Of those that a mesh axis runs over, the one named last changes fastest.
Arguments:
- features: bfloat16 [3072, 2048], P('dp'), may hold values from -128 to 128
- labels: int32 [3072], P('dp'), may hold values from 0 to 16383
- weight: bfloat16 [2048, 16384], P('dp', 'cls'), may hold values from -1 to 1
- noise: float32 [16, 2, 1024, 1024], P('dp', 'cls'), may hold values from -6 to 6
Outputs:
- noisy_grad: float32 [16, 2, 1024, 1024], P('dp', 'cls')
All inputs are finite; a program needn't handle non-finite values.
Results may differ from a plain program's by a relative error of at most 0.0017.
Values may be sent and summed in bfloat16 or wider, within the bound.
A program may use at most 128 MiB of HBM per device.

v0:
```python
import jax
import jax.numpy as jnp
from jax import lax
from jax.sharding import PartitionSpec as P

CSPLIT = 8


CLIP_NORM = 40.0
NOISE_STD = 0.4


def on_device(features, labels, weight, noise):
    tok_rows = features.shape[0]
    feature_dim = features.shape[1]
    class_shard = weight.shape[1]
    groups = lax.axis_size("dp") // CSPLIT
    row_block = feature_dim // groups
    col_block = class_shard // CSPLIT
    slot_count = groups * CSPLIT
    feature_slots = jnp.broadcast_to(
        features.reshape(tok_rows, groups, 1, row_block), (tok_rows, groups, CSPLIT, row_block)
    ).reshape(tok_rows, slot_count, row_block)
    logits = jnp.dot(
        features,
        lax.all_gather(weight, "dp", axis=0, tiled=True),
        preferred_element_type=jnp.float32,
    )
    offset = labels - lax.axis_index("cls") * class_shard
    label_hit = lax.broadcasted_iota(jnp.int32, (tok_rows, class_shard), 1) == offset[:, None]
    onehot = label_hit.astype(jnp.float32)
    local_max = jnp.max(logits, axis=1)
    exponent = jnp.exp(logits - local_max[:, None])
    row_total = jnp.sum(exponent, axis=1)
    row_square = jnp.sum(exponent * exponent, axis=1)
    picked = jnp.sum(onehot * logits, axis=1)
    global_max = lax.pmax(local_max, "cls")
    rescale = jnp.exp(local_max - global_max)
    row_total, row_square, picked = lax.psum(
        (row_total * rescale, row_square * rescale * rescale, picked), "cls"
    )
    softmax = exponent * (jnp.exp(local_max - global_max) / row_total)[:, None]
    label_prob = jnp.exp(picked - global_max) / row_total
    spread = row_square / (row_total * row_total) - 2.0 * label_prob + 1.0
    energy = jnp.sum(jnp.square(features.astype(jnp.float32)), axis=1)
    factor = CLIP_NORM * lax.rsqrt(jnp.maximum(energy * spread, CLIP_NORM * CLIP_NORM))
    weighted = (factor[:, None] * (softmax - onehot)).astype(jnp.bfloat16)
    coef_slots = jnp.broadcast_to(
        weighted.reshape(tok_rows, 1, CSPLIT, col_block), (tok_rows, groups, CSPLIT, col_block)
    ).reshape(tok_rows, slot_count, col_block)
    feature_recv, coef_recv = (
        lax.all_to_all(feature_slots, "dp", split_axis=1, concat_axis=1, tiled=True),
        lax.all_to_all(coef_slots, "dp", split_axis=1, concat_axis=1, tiled=True),
    )
    grad_block = lax.dot_general(
        feature_recv, coef_recv, (((0, 1), (0, 1)), ((), ())), preferred_element_type=jnp.float32
    )
    return (grad_block + NOISE_STD * noise[0, 0]).reshape(noise.shape)


def solution(mesh):
    placed = (P("dp", None), P("dp"), P("dp", "cls"), P("dp", "cls", None, None))
    return jax.shard_map(
        on_device, mesh=mesh, in_specs=placed, out_specs=P("dp", "cls", None, None), check_vma=False
    )
```

profile of v0, /device:TPU:28, one launch (start us, length us, event | category | flops | bytes accessed | tf_op | source)
XLA Modules:
  0.0 691.1 jit_solution(1169559670547436324)
XLA Ops:
  6.5 0.0 all-gather.2.cloned.1.call-start
  6.5 0.7 all-gather.2.cloned.1.call-update
  7.3 1.2 copy.14
  8.5 3.4 broadcast_in_dim.21
  11.8 0.0 copy-start
  11.9 0.0 copy-start.1
  11.9 7.1 %all-to-all-start.1 = ((bf16[192,16,1024]{2,0,1:T(8,128)(2,1)}), bf16[192,16,1024]{2,0,1:T(8,128)(2,1)}, u32[]{:S(2)}, u32[]{:S(2)}) async-start(bf16[192,16,1024]{2,0,1:T(8,128)(2,1)} %bitcast.24), calls=%async_computation.1 | async-start | bytes 12582912 | tf_op jit(solution)/shard_map/all_to_all | solution.py:52
  18.9 0.0 copy-done
  18.9 0.2 multiply_reduce_fusion.1
  19.2 0.0 copy-done.1
  19.2 463.0 %all-gather.2.cloned.1.call-done = bf16[2048,8192]{1,0:T(8,128)(2,1)} async-done(((bf16[128,8192]{1,0:T(8,128)(2,1)}), bf16[2048,8192]{1,0:T(8,128)(2,1)}) %all-gather.2.cloned.1.call-update) | async-done | bytes 33554448 | tf_op jit(solution)/shard_map/all_gather | solution.py:26
  482.2 16.4 %fusion.4 = (f32[192]{0:T(256)S(1)}, f32[192,8192]{1,0:T(8,128)}) fusion(bf16[192,2048]{1,0:T(8,128)(2,1)S(1)} %copy-done, bf16[2048,8192]{1,0:T(8,128)(2,1)} %all-gather.2.cloned.1.call-done), kind=kOutput, calls=%fused_computation.18 | convolution fusion | flops 6444023808 | bytes 40633088 | tf_op jit(solution)/shard_map/dot_general | solution.py:24
  498.6 2.4 pmax.7
  501.1 4.2 multiply_reduce_fusion
  505.3 2.5 all-reduce
  507.8 4.0 multiply_convert_fusion
  511.8 0.4 copy.13
  512.2 0.0 all-to-all-done.1
  512.2 3.6 broadcast_in_dim.9
  515.9 6.8 all-to-all-start
  522.7 5.3 copy.7
  528.1 138.2 %all-to-all-done = bf16[192,16,1024]{2,0,1:T(8,128)(2,1)} async-done(((bf16[192,16,1024]{2,0,1:T(8,128)(2,1)}), bf16[192,16,1024]{2,0,1:T(8,128)(2,1)}, u32[]{:S(2)}, u32[]{:S(2)}) %all-to-all-start) | async-done | bytes 6291488 | tf_op jit(solution)/shard_map/all_to_all | solution.py:53
  666.3 12.7 %fusion.1 = f32[1,1,1024,1024]{2,3,1,0:T(8,128)} fusion(f32[1,1,1024,1024]{2,3,1,0:T(8,128)} %copy.7, bf16[192,16,1024]{2,0,1:T(8,128)(2,1)} %all-to-all-done, bf16[192,16,1024]{2,0,1:T(8,128)(2,1)} %all-to-all-done.1), kind=kOutput, calls=%fused_computation.7 | convolution fusion | flops 6444548096 | bytes 20971520 | tf_op jit(solution)/shard_map/dot_general | solution.py:55
  679.0 5.3 copy.8
  (3 shorter events, 0.0 us)
Async XLA Ops:
  6.5 475.7 %all-gather.2.cloned.1.call-start = ((), (), s32[]{:S(2)}) async-start(), calls=%async_computation.2 | async-start | bytes 35651584 | tf_op jit(solution)/shard_map/all_gather | solution.py:26
  11.8 7.1 %copy-start = (bf16[192,2048]{1,0:T(8,128)(2,1)S(1)}, bf16[192,2048]{1,0:T(8,128)(2,1)}, u32[]{:S(2)}) copy-start(bf16[192,2048]{1,0:T(8,128)(2,1)} %param.4) | copy-start | bytes 2359300
  11.9 7.3 %copy-start.1 = (s32[192]{0:T(256)S(1)}, s32[192]{0:T(256)}, u32[]{:S(2)}) copy-start(s32[192]{0:T(256)} %param.5) | copy-start | bytes 2308
  11.9 500.4 %all-to-all-start.1 = ((bf16[192,16,1024]{2,0,1:T(8,128)(2,1)}), bf16[192,16,1024]{2,0,1:T(8,128)(2,1)}, u32[]{:S(2)}, u32[]{:S(2)}) async-start(bf16[192,16,1024]{2,0,1:T(8,128)(2,1)} %bitcast.24), calls=%async_computation.1 | async-start | bytes 12582912 | tf_op jit(solution)/shard_map/all_to_all | solution.py:52
  515.9 150.4 %all-to-all-start = ((bf16[192,16,1024]{2,0,1:T(8,128)(2,1)}), bf16[192,16,1024]{2,0,1:T(8,128)(2,1)}, u32[]{:S(2)}, u32[]{:S(2)}) async-start(bf16[192,16,1024]{2,0,1:T(8,128)(2,1)} %bitcast.25), calls=%async_computation | async-start | bytes 12582912 | tf_op jit(solution)/shard_map/all_to_all | solution.py:53
Sparse Core Ops, SparseCore 0:
  10.1 472.0 all-gather.1
where the time goes:
time: 692 us; the launch traced here: 691 us
  waiting for transfers between devices  602 us (87%)
  matrix products  29.1 us (4%)
  local copies, waits for them, and re-layouts  19.3 us (3%)
  starting transfers between devices  13.9 us (2%)
  between operations  13.4 us (2%)
  other arithmetic  8.47 us (1%)
    all_gather x1, waiting for transfers between devices, on_device(): lax.all_gather(weight, 'dp', axis=0, tiled=True)  463 us
    all_to_all x1, waiting for transfers between devices, on_device(): lax.all_to_all(coef_slots, 'dp', split_axis=1, concat_axis=1, tiled=True)  138 us
    dot_general x1, matrix products, on_device(): jnp.dot(features, lax.all_gather(weight, 'dp', axis=0, tiled=True), prefe...  16.4 us
  transfers between devices with their start and end apart: 3, of which 2 were waited for; matrix products, arithmetic and copies ran while one was open for 5% of the time, Pallas kernels for 0%

commit v1 on v0

--- a/solution.py
+++ b/solution.py
@@ -1,16 +1,145 @@
+import functools
+
 import jax
 import jax.numpy as jnp
 from jax import lax
+from jax.experimental import pallas as pl
+from jax.experimental.pallas import tpu as pltpu
 from jax.sharding import PartitionSpec as P
 
 CSPLIT = 8
-
-
 CLIP_NORM = 40.0
 NOISE_STD = 0.4
-
-
-def on_device(features, labels, weight, noise):
+GATHER_LIMIT = 16 << 20
+MESH = pl.DeviceIdType.MESH
+
+
+def exchange_kernel(n_dp, feat_ref, weight_ref, feats_ref, wcols_ref,
+                    send_sem, sib_send_sem, recv_sem, sib_recv_sem, wsend_sem, wrecv_sem, local_sem):
+    me = lax.axis_index("dp")
+    cls = lax.axis_index("cls")
+    core = cls % 2
+    sibling = cls + 1 - 2 * core
+    stages = n_dp.bit_length() - 1
+    rows = feat_ref.shape[0]
+    half = rows // 2
+    cols = wcols_ref.shape[2]
+
+    barrier = pltpu.get_barrier_semaphore()
+    for hop in range(1, n_dp):
+        pl.semaphore_signal(barrier, inc=1, device_id=((me + hop) % n_dp, cls), device_id_type=MESH)
+    pl.semaphore_signal(barrier, inc=1, device_id=(me, sibling), device_id_type=MESH)
+    pl.semaphore_wait(barrier, n_dp)
+
+    bit_step = [(1 << b) * (1 - 2 * ((me // (1 << b)) % 2)) for b in range(stages)]
+
+    def stage_steps(which):
+        steps = [bit_step[b] for b in range(stages - 1, 1, -1)]
+        return steps + [bit_step[1] * (1 - which) + bit_step[0] * which,
+                        bit_step[0] * (1 - which) + bit_step[1] * which]
+
+    steps = stage_steps(core)
+    sib_steps = stage_steps(1 - core)
+
+    def origin(mask, table):
+        spot = me
+        for s in range(stages):
+            if mask >> s & 1:
+                spot = spot + table[s]
+        return spot
+
+    mine = pl.ds(pl.multiple_of(core * half, half), half)
+    other = pl.ds(pl.multiple_of((1 - core) * half, half), half)
+    sends = []
+
+    def forward(mask, source, slot):
+        first = mask.bit_length()
+        for s in range(first, stages):
+            copy = pltpu.make_async_remote_copy(
+                src_ref=source,
+                dst_ref=feats_ref.at[slot, mine],
+                send_sem=send_sem.at[mask * stages + s],
+                recv_sem=recv_sem.at[mask | 1 << s],
+                device_id=(me + steps[s], cls),
+                device_id_type=MESH,
+            )
+            copy.start()
+            sends.append(copy)
+        if mask:
+            copy = pltpu.make_async_remote_copy(
+                src_ref=source,
+                dst_ref=feats_ref.at[slot, mine],
+                send_sem=sib_send_sem.at[mask],
+                recv_sem=sib_recv_sem.at[mask],
+                device_id=(me, sibling),
+                device_id_type=MESH,
+            )
+            copy.start()
+            sends.append(copy)
+
+    forward(0, feat_ref.at[mine], me)
+    keep = [
+        pltpu.make_async_copy(feat_ref, feats_ref.at[me], local_sem.at[0]),
+        pltpu.make_async_copy(
+            weight_ref.at[:, pl.ds(pl.multiple_of(me % CSPLIT * cols, cols), cols)],
+            wcols_ref.at[me], local_sem.at[1]),
+    ]
+    for copy in keep:
+        copy.start()
+    for hop in range(1, n_dp):
+        peer = (me + hop) % n_dp
+        copy = pltpu.make_async_remote_copy(
+            src_ref=weight_ref.at[:, pl.ds(pl.multiple_of(peer % CSPLIT * cols, cols), cols)],
+            dst_ref=wcols_ref.at[me],
+            send_sem=wsend_sem.at[hop],
+            recv_sem=wrecv_sem.at[hop],
+            device_id=(peer, cls),
+            device_id_type=MESH,
+        )
+        copy.start()
+        sends.append(copy)
+
+    def arrived(ref, sem):
+        pltpu.make_async_remote_copy(
+            src_ref=ref, dst_ref=ref, send_sem=sem, recv_sem=sem,
+            device_id=(me, sibling), device_id_type=MESH,
+        ).wait_recv()
+
+    for mask in range(1, n_dp):
+        slot = origin(mask, steps)
+        arrived(feats_ref.at[slot, mine], recv_sem.at[mask])
+        forward(mask, feats_ref.at[slot, mine], slot)
+    for mask in range(1, n_dp):
+        arrived(feats_ref.at[origin(mask, sib_steps), other], sib_recv_sem.at[mask])
+    for hop in range(1, n_dp):
+        arrived(wcols_ref.at[(me + n_dp - hop) % n_dp], wrecv_sem.at[hop])
+    for copy in keep:
+        copy.wait()
+    for copy in sends:
+        copy.wait_send()
+
+
+def exchange(features, weight, n_dp, col_block):
+    stages = n_dp.bit_length() - 1
+    anywhere = pl.BlockSpec(memory_space=pl.ANY)
+    dma = pltpu.SemaphoreType.DMA
+    return pl.pallas_call(
+        functools.partial(exchange_kernel, n_dp),
+        out_shape=(
+            jax.ShapeDtypeStruct((n_dp,) + features.shape, features.dtype),
+            jax.ShapeDtypeStruct((n_dp, weight.shape[0], col_block), weight.dtype),
+        ),
+        in_specs=[anywhere] * 2,
+        out_specs=(anywhere, anywhere),
+        scratch_shapes=[
+            dma((n_dp * stages,)), dma((n_dp,)), dma((n_dp,)), dma((n_dp,)),
+            dma((n_dp,)), dma((n_dp,)), dma((2,)),
+        ],
+        compiler_params=pltpu.CompilerParams(collective_id=0, has_side_effects=True),
+    )(features, weight)
+
+
+def examples_split(features, labels, weight, noise):
     tok_rows = features.shape[0]
     feature_dim = features.shape[1]
     class_shard = weight.shape[1]
@@ -58,6 +187,51 @@
     return (grad_block + NOISE_STD * noise[0, 0]).reshape(noise.shape)
 
 
+def on_device(features, labels, weight, noise):
+    n_dp = lax.axis_size("dp")
+    if n_dp * features.size * features.dtype.itemsize > GATHER_LIMIT:
+        return examples_split(features, labels, weight, noise)
+    feature_dim = features.shape[1]
+    class_shard = weight.shape[1]
+    groups = n_dp // CSPLIT
+    row_block = feature_dim // groups
+    col_block = class_shard // CSPLIT
+    me = lax.axis_index("dp")
+
+    own_energy = jnp.sum(jnp.square(features.astype(jnp.float32)), axis=1)
+    energy = lax.all_gather(own_energy, "dp", axis=0, tiled=True)
+    all_labels = lax.all_gather(labels, "dp", axis=0, tiled=True)
+    feats, wcols = exchange(features, weight, n_dp, col_block)
+    feats = feats.reshape(-1, feature_dim)
+    wcols = wcols.reshape(feature_dim, col_block)
+
+    logits = jnp.dot(feats, wcols, preferred_element_type=jnp.float32)
+    offset = all_labels - (lax.axis_index("cls") * class_shard + me % CSPLIT * col_block)
+    hit = lax.broadcasted_iota(jnp.int32, logits.shape, 1) == offset[:, None]
+    local_max = jnp.max(logits, axis=1)
+    exponent = jnp.exp(logits - local_max[:, None])
+    stats = jnp.stack([
+        local_max,
+        jnp.sum(exponent, axis=1),
+        jnp.sum(exponent * exponent, axis=1),
+        jnp.sum(jnp.where(hit, logits, 0.0), axis=1),
+    ])
+    gathered = lax.all_gather(stats, ("dp", "cls"), axis=0, tiled=False)
+    gathered = gathered.reshape((groups, -1) + stats.shape)[0]
+    row_max = jnp.max(gathered[:, 0], axis=0)
+    rescale = jnp.exp(gathered[:, 0] - row_max)
+    row_total = jnp.sum(gathered[:, 1] * rescale, axis=0)
+    row_square = jnp.sum(gathered[:, 2] * rescale * rescale, axis=0)
+    picked = jnp.sum(gathered[:, 3], axis=0)
+    spread = row_square / (row_total * row_total) - 2.0 * jnp.exp(picked - row_max) / row_total + 1.0
+    factor = CLIP_NORM * lax.rsqrt(jnp.maximum(energy * spread, CLIP_NORM * CLIP_NORM))
+    scale = jnp.exp(local_max - row_max) / row_total
+    coef = (factor[:, None] * (exponent * scale[:, None] - hit.astype(jnp.float32))).astype(jnp.bfloat16)
+    feat_rows = lax.dynamic_slice_in_dim(feats, me // CSPLIT * row_block, row_block, axis=1)
+    grad = lax.dot_general(feat_rows, coef, (((0,), (0,)), ((), ())), preferred_element_type=jnp.float32)
+    return (grad + NOISE_STD * noise[0, 0]).reshape(noise.shape)
+
+
 def solution(mesh):
     placed = (P("dp", None), P("dp"), P("dp", "cls"), P("dp", "cls", None, None))
     return jax.shard_map(

time: 692 us -> 350 us (0.51)
  the two profiles are of different devices: /device:TPU:28 before, /device:TPU:0 now
where the time goes in v1:
time: 350 us; the launch traced here: 349 us
  blocking collectives  177 us (51%)
  Pallas kernels  112 us (32%)
  matrix products  31.7 us (9%)
  between operations  14.1 us (4%)
  other arithmetic  8.22 us (2%)
  local copies, waits for them, and re-layouts  6.87 us (2%)
    unnamed x2, blocking collectives  177 us
    pallas_call x1, Pallas kernels, exchange(): pl.pallas_call(functools.partial(exchange_kernel, n_dp), out_shape=(jax.S...  112 us
    dot_general x1, matrix products, on_device(): logits = jnp.dot(feats, wcols, preferred_element_type=jnp.float32)  17.9 us
    dot_general x1, matrix products, on_device(): lax.dot_general(feat_rows, coef, (((0,), (0,)), ((), ())), preferred_elem...  13.7 us
  transfers between devices with their start and end apart: 1, of which 0 were waited for; matrix products, arithmetic and copies ran while one was open for 0% of the time, Pallas kernels for 0%

profile of v1, /device:TPU:0, one launch (start us, length us, event | category | flops | bytes accessed | tf_op | source)
XLA Modules:
  0.0 349.4 jit_solution(17858236980275890969)
XLA Ops:
  6.5 0.0 all-gather.4.cloned.1.call-start
  6.5 1.2 dynamic-slice
  8.4 0.9 dynamic-update-slice.1
  9.3 79.2 %all-reduce.1 = s32[3072]{0:T(1024)S(1)} all-reduce(s32[3072]{0:T(1024)S(1)} %dynamic-update-slice.1), channel_id=1, replica_groups=mesh['dp'=16,'cls'=2] {'dp'}, use_global_device_ids=true, to_apply=%add.1 | all-reduce | flops 3072 | bytes 24576
  88.6 111.7 %shard_map.46 = (bf16[16,192,2048]{2,1,0:T(8,128)(2,1)}, bf16[16,128,1024]{2,1,0:T(8,128)(2,1)}) custom-call(bf16[192,2048]{1,0:T(8,128)(2,1)} %feat_ref.1, bf16[128,8192]{1,0:T(8,128)(2,1)} %weight_ref.1), custom_call_target="tpu_custom_call" | custom-call | tf_op jit(solution)/shard_map/pallas_call | solution.py:126
  200.3 17.9 %fusion.16 = (f32[3072]{0:T(1024)S(1)}, f32[3072,1024]{0,1:T(8,128)S(1)}) fusion(bf16[3072,2048]{1,0:T(8,128)(2,1)} %bitcast.39, bf16[2048,1024]{1,0:T(8,128)(2,1)} %bitcast.41), kind=kOutput, calls=%fused_computation.31 | convolution fusion | flops 12888044544 | bytes 29372416 | tf_op jit(solution)/shard_map/dot_general | solution.py:208
  218.3 0.0 copy-start
  218.3 0.0 copy-start.1
  218.3 4.5 %copy-done = f32[3072,1024]{0,1:T(8,128)} copy-done((f32[3072,1024]{0,1:T(8,128)}, f32[3072,1024]{0,1:T(8,128)S(1)}, u32[]{:S(2)}) %copy-start) | copy-done | bytes 12582936
  222.7 4.1 %fusion = (f32[3072]{0:T(1024)S(1)}, f32[3072]{0:T(1024)S(1)}, f32[3072]{0:T(1024)S(1)}) fusion(f32[3072,1024]{0,1:T(8,128)S(1)} %get-tuple-element.24, f32[3072]{0:T(1024)S(1)} %get-tuple-element.23, s32[3072]{0:T(1024)S(1)} %broadcast_subtract_fusion), kind=kLoop, calls=%fused_computation.5 | loop fusion | flops 22010880 | bytes 12644352 | tf_op jit(solution)/shard_map/reduce_sum | solution.py:215
  226.8 0.7 maximum_bitcast_fusion
  227.5 0.0 all-gather.4.cloned.1.call-update
  227.6 0.0 copy-done.1
  227.6 0.2 multiply_reduce_fusion.1
  227.8 0.3 dynamic-update-slice
  228.1 97.5 %all-reduce = f32[3072]{0:T(1024)S(1)} all-reduce(f32[3072]{0:T(1024)S(1)} %dynamic-update-slice), channel_id=1, replica_groups=mesh['dp'=16,'cls'=2] {'dp'}, use_global_device_ids=true, to_apply=%add | all-reduce | flops 3072 | bytes 24576
  325.6 0.0 all-gather.4.cloned.1.call-done
  325.6 3.0 fusion.15
  328.6 0.1 fusion.10
  328.8 13.7 %fusion.7 = f32[1,1,1024,1024]{3,2,1,0:T(8,128)} fusion(f32[1,1,1024,1024]{3,2,1,0:T(8,128)} %param.7, f32[3072,1024]{0,1:T(8,128)} %copy-done, f32[3072]{0:T(1024)S(1)} %get-tuple-element.22, f32[3072]{0:T(1024)S(1)} %get-tuple-element.21, s32[3072]{0:T(1024)S(1)} %broadcast_subtract_fusion, f32[3072]{0:T(1024)S(1)} %get-tuple-element.23, ...), kind=kOutput, calls=%fused_computation.13 | convolution fusion | flops 6466568192 | bytes 27312132 | tf_op jit(solution)/shard_map/dot_general | solution.py:231
  (4 shorter events, 0.0 us)
Async XLA Ops:
  6.5 319.1 %all-gather.4.cloned.1.call-start = ((), (), s32[]{:S(2)}) async-start(), calls=%async_computation | async-start | bytes 1622016 | tf_op jit(solution)/shard_map/all_gather | solution.py:219
  218.3 4.5 %copy-start = (f32[3072,1024]{0,1:T(8,128)}, f32[3072,1024]{0,1:T(8,128)S(1)}, u32[]{:S(2)}) copy-start(f32[3072,1024]{0,1:T(8,128)S(1)} %get-tuple-element.24) | copy-start | bytes 37748740
  218.3 9.3 %copy-start.1 = (bf16[192,2048]{1,0:T(8,128)(2,1)S(1)}, bf16[192,2048]{1,0:T(8,128)(2,1)}, u32[]{:S(2)}) copy-start(bf16[192,2048]{1,0:T(8,128)(2,1)} %feat_ref.1) | copy-start | bytes 2359300
Sparse Core Ops, SparseCore 0:
  227.7 82.9 all-gather.3

commit v2 on v1

--- a/solution.py
+++ b/solution.py
@@ -14,8 +14,8 @@
 MESH = pl.DeviceIdType.MESH
 
 
-def exchange_kernel(n_dp, feat_ref, weight_ref, feats_ref, wcols_ref,
-                    send_sem, sib_send_sem, recv_sem, sib_recv_sem, wsend_sem, wrecv_sem, local_sem):
+def exchange_kernel(n_dp, feat_ref, weight_ref, side_ref, feats_ref, wcols_ref, sides_ref,
+                    send_sem, sib_send_sem, recv_sem, sib_recv_sem, wsend_sem, wrecv_sem, ssend_sem, srecv_sem, local_sem):
     me = lax.axis_index("dp")
     cls = lax.axis_index("cls")
     core = cls % 2
@@ -83,6 +83,7 @@
         pltpu.make_async_copy(
             weight_ref.at[:, pl.ds(pl.multiple_of(me % CSPLIT * cols, cols), cols)],
             wcols_ref.at[me], local_sem.at[1]),
+        pltpu.make_async_copy(side_ref, sides_ref.at[me], local_sem.at[2]),
     ]
     for copy in keep:
         copy.start()
@@ -98,6 +99,16 @@
         )
         copy.start()
         sends.append(copy)
+        copy = pltpu.make_async_remote_copy(
+            src_ref=side_ref,
+            dst_ref=sides_ref.at[me],
+            send_sem=ssend_sem.at[hop],
+            recv_sem=srecv_sem.at[hop],
+            device_id=(peer, cls),
+            device_id_type=MESH,
+        )
+        copy.start()
+        sends.append(copy)
 
     def arrived(ref, sem):
         pltpu.make_async_remote_copy(
@@ -113,13 +124,14 @@
         arrived(feats_ref.at[origin(mask, sib_steps), other], sib_recv_sem.at[mask])
     for hop in range(1, n_dp):
         arrived(wcols_ref.at[(me + n_dp - hop) % n_dp], wrecv_sem.at[hop])
+        arrived(sides_ref.at[(me + n_dp - hop) % n_dp], srecv_sem.at[hop])
     for copy in keep:
         copy.wait()
     for copy in sends:
         copy.wait_send()
 
 
-def exchange(features, weight, n_dp, col_block):
+def exchange(features, weight, side, n_dp, col_block):
     stages = n_dp.bit_length() - 1
     anywhere = pl.BlockSpec(memory_space=pl.ANY)
     dma = pltpu.SemaphoreType.DMA
@@ -128,15 +140,67 @@
         out_shape=(
             jax.ShapeDtypeStruct((n_dp,) + features.shape, features.dtype),
             jax.ShapeDtypeStruct((n_dp, weight.shape[0], col_block), weight.dtype),
+            jax.ShapeDtypeStruct((n_dp,) + side.shape, side.dtype),
         ),
-        in_specs=[anywhere] * 2,
-        out_specs=(anywhere, anywhere),
+        in_specs=[anywhere] * 3,
+        out_specs=(anywhere,) * 3,
         scratch_shapes=[
             dma((n_dp * stages,)), dma((n_dp,)), dma((n_dp,)), dma((n_dp,)),
-            dma((n_dp,)), dma((n_dp,)), dma((2,)),
+            dma((n_dp,)), dma((n_dp,)), dma((n_dp,)), dma((n_dp,)), dma((3,)),
         ],
         compiler_params=pltpu.CompilerParams(collective_id=0, has_side_effects=True),
-    )(features, weight)
+    )(features, weight, side)
+
+
+def stats_kernel(n_cls, stats_ref, all_ref, send_sem, recv_sem):
+    me = lax.axis_index("dp")
+    cls = lax.axis_index("cls")
+    first = me // CSPLIT * CSPLIT
+    count = CSPLIT * n_cls
+    place = me % CSPLIT * n_cls + cls
+
+    def peer(hop):
+        spot = (place + hop) % count
+        return (first + spot // n_cls, spot % n_cls)
+
+    barrier = pltpu.get_barrier_semaphore()
+    for hop in range(1, count):
+        pl.semaphore_signal(barrier, inc=1, device_id=peer(hop), device_id_type=MESH)
+    pl.semaphore_wait(barrier, count - 1)
+    copies = []
+    for hop in range(1, count):
+        copy = pltpu.make_async_remote_copy(
+            src_ref=stats_ref,
+            dst_ref=all_ref.at[place],
+            send_sem=send_sem.at[hop],
+            recv_sem=recv_sem.at[hop],
+            device_id=peer(hop),
+            device_id_type=MESH,
+        )
+        copy.start()
+        copies.append(copy)
+    all_ref[pl.ds(place, 1)] = stats_ref[...][None]
+    for hop in range(1, count):
+        spot = all_ref.at[(place + count - hop) % count]
+        pltpu.make_async_remote_copy(
+            src_ref=spot, dst_ref=spot, send_sem=send_sem.at[hop], recv_sem=recv_sem.at[hop],
+            device_id=peer(hop), device_id_type=MESH,
+        ).wait_recv()
+    for copy in copies:
+        copy.wait_send()
+
+
+def gather_stats(stats, n_cls):
+    count = CSPLIT * n_cls
+    inside = pl.BlockSpec(memory_space=pltpu.VMEM)
+    return pl.pallas_call(
+        functools.partial(stats_kernel, n_cls),
+        out_shape=jax.ShapeDtypeStruct((count,) + stats.shape, stats.dtype),
+        in_specs=[inside],
+        out_specs=inside,
+        scratch_shapes=[pltpu.SemaphoreType.DMA((count,)), pltpu.SemaphoreType.DMA((count,))],
+        compiler_params=pltpu.CompilerParams(collective_id=1, has_side_effects=True),
+    )(stats)
 
 
 def examples_split(features, labels, weight, noise):
@@ -199,9 +263,10 @@
     me = lax.axis_index("dp")
 
     own_energy = jnp.sum(jnp.square(features.astype(jnp.float32)), axis=1)
-    energy = lax.all_gather(own_energy, "dp", axis=0, tiled=True)
-    all_labels = lax.all_gather(labels, "dp", axis=0, tiled=True)
-    feats, wcols = exchange(features, weight, n_dp, col_block)
+    side = jnp.stack([labels.astype(jnp.float32), own_energy])
+    feats, wcols, sides = exchange(features, weight, side, n_dp, col_block)
+    all_labels = sides[:, 0].reshape(-1).astype(jnp.int32)
+    energy = sides[:, 1].reshape(-1)
     feats = feats.reshape(-1, feature_dim)
     wcols = wcols.reshape(feature_dim, col_block)
 
@@ -216,8 +281,7 @@
         jnp.sum(exponent * exponent, axis=1),
         jnp.sum(jnp.where(hit, logits, 0.0), axis=1),
     ])
-    gathered = lax.all_gather(stats, ("dp", "cls"), axis=0, tiled=False)
-    gathered = gathered.reshape((groups, -1) + stats.shape)[0]
+    gathered = gather_stats(stats, lax.axis_size("cls"))
     row_max = jnp.max(gathered[:, 0], axis=0)
     rescale = jnp.exp(gathered[:, 0] - row_max)
     row_total = jnp.sum(gathered[:, 1] * rescale, axis=0)

time: 350 us -> 215 us (0.61)
  the two profiles are of different devices: /device:TPU:0 before, /device:TPU:7 now
where the time goes in v2:
time: 215 us; the launch traced here: 214 us
  Pallas kernels  166 us (77%)
  matrix products  31.6 us (15%)
  other arithmetic  11.4 us (5%)
  local copies, waits for them, and re-layouts  5.42 us (3%)
    pallas_call x1, Pallas kernels, exchange(): pl.pallas_call(functools.partial(exchange_kernel, n_dp), out_shape=(jax.S...  139 us
    pallas_call x1, Pallas kernels, gather_stats(): pl.pallas_call(functools.partial(stats_kernel, n_cls), out_shape=jax.Shap...  26.7 us
    dot_general x1, matrix products, on_device(): logits = jnp.dot(feats, wcols, preferred_element_type=jnp.float32)  17.9 us
    dot_general x1, matrix products, on_device(): lax.dot_general(feat_rows, coef, (((0,), (0,)), ((), ())), preferred_elem...  13.7 us
    unnamed x2, local copies, waits for them, and re-layouts  4.46 us

profile of v2, /device:TPU:7, one launch (start us, length us, event | category | flops | bytes accessed | tf_op | source)
XLA Modules:
  0.0 214.4 jit_solution(8039442342306192695)
XLA Ops:
  0.0 0.7 convert_element_type.20
  0.7 1.4 multiply_reduce_fusion.1
  2.1 0.6 pad_maximum_fusion.1.side_ref
  2.6 139.1 %shard_map.46 = (bf16[16,192,2048]{2,1,0:T(8,128)(2,1)}, bf16[16,128,1024]{2,1,0:T(8,128)(2,1)}, f32[16,2,192]{2,1,0:T(2,128)}) custom-call(bf16[192,2048]{1,0:T(8,128)(2,1)} %feat_ref.1, bf16[128,8192]{1,0:T(8,128)(2,1)} %weight_ref.1, f32[2,192]{1,0:T(2,128)} %pad_maximum_fusion.1.side_ref), custom_call_target="tpu_custom_call" | custom-call | tf_op jit(solution)/shard_map/pallas_call | solution.py:138
  141.8 0.8 subtract_reduce_fusion
  142.6 0.8 slice_reduce_fusion.1
  143.4 0.1 sub.62
  143.5 0.1 reshape_squeeze.4
  143.5 17.9 %fusion.16 = (f32[3072]{0:T(1024)S(1)}, f32[3072,1024]{0,1:T(8,128)S(1)}) fusion(bf16[3072,2048]{1,0:T(8,128)(2,1)} %bitcast.40, bf16[2048,1024]{1,0:T(8,128)(2,1)} %bitcast.42), kind=kOutput, calls=%fused_computation.33 | convolution fusion | flops 12888044544 | bytes 29372416 | tf_op jit(solution)/shard_map/dot_general | solution.py:273
  161.5 0.0 copy-start
  161.5 4.5 %copy-done = f32[3072,1024]{0,1:T(8,128)} copy-done((f32[3072,1024]{0,1:T(8,128)}, f32[3072,1024]{0,1:T(8,128)S(1)}, u32[]{:S(2)}) %copy-start) | copy-done | bytes 12582936
  166.0 4.1 %fusion = (f32[3072]{0:T(1024)S(1)}, f32[3072]{0:T(1024)S(1)}, f32[3072]{0:T(1024)S(1)}) fusion(f32[3072,1024]{0,1:T(8,128)S(1)} %get-tuple-element.26, f32[3072]{0:T(1024)S(1)} %get-tuple-element.25, s32[3072]{0:T(1024)S(1)} %sub.62), kind=kLoop, calls=%fused_computation.5 | loop fusion | flops 22010880 | bytes 12644352 | tf_op jit(solution)/shard_map/reduce_sum | solution.py:280
  170.1 0.7 pad_maximum_fusion.stats_ref
  170.7 26.7 %shard_map.47 = f32[16,4,3072]{2,1,0:T(4,128)} custom-call(f32[4,3072]{1,0:T(4,128)} %pad_maximum_fusion.stats_ref), custom_call_target="tpu_custom_call" | custom-call | tf_op jit(solution)/shard_map/pallas_call | solution.py:196
  197.4 3.0 %fusion.15 = (f32[16,1,3072]{2,1,0:T(1,128)S(1)}, f32[16,1,3072]{2,1,0:T(1,128)S(1)}, f32[3072]{0:T(1024)S(1)}, f32[3072]{0:T(1024)S(1)}, f32[16,1,3072]{2,1,0:T(1,128)S(1)}) fusion(f32[16,4,3072]{2,1,0:T(4,128)} %shard_map.47), kind=kLoop, calls=%fused_computation.32 | loop fusion | flops 92160 | bytes 1400832 | tf_op jit(solution)/shard_map/slice | solution.py:287
  200.5 0.1 fusion.10
  200.7 13.7 %fusion.7 = f32[1,1,1024,1024]{3,2,1,0:T(8,128)} fusion(f32[1,1,1024,1024]{3,2,1,0:T(8,128)} %param.7, f32[3072,1024]{0,1:T(8,128)} %copy-done, f32[3072]{0:T(1024)S(1)} %get-tuple-element.24, f32[3072]{0:T(1024)S(1)} %get-tuple-element.23, s32[3072]{0:T(1024)S(1)} %sub.62, f32[3072]{0:T(1024)S(1)} %get-tuple-element.25, bf16[3072,2048]{1,0:T(8,128)(2,1)} %bitcast.41, ...), kind=kOutput, calls=%fused_computation.13 | convolution fusion | flops 6466568192 | bytes 27312132 | tf_op jit(solution)/shard_map/dot_general | solution.py:295
  (1 shorter events, 0.0 us)
Async XLA Ops:
  161.5 4.5 %copy-start = (f32[3072,1024]{0,1:T(8,128)}, f32[3072,1024]{0,1:T(8,128)S(1)}, u32[]{:S(2)}) copy-start(f32[3072,1024]{0,1:T(8,128)S(1)} %get-tuple-element.26) | copy-start | bytes 37748740

commit v3 on v0

--- a/solution.py
+++ b/solution.py
@@ -1,16 +1,282 @@
+import functools
+
 import jax
 import jax.numpy as jnp
 from jax import lax
+from jax.experimental import pallas as pl
+from jax.experimental.pallas import tpu as pltpu
 from jax.sharding import PartitionSpec as P
 
 CSPLIT = 8
-
-
 CLIP_NORM = 40.0
 NOISE_STD = 0.4
-
-
-def on_device(features, labels, weight, noise):
+GATHER_LIMIT = 16 << 20
+CHUNKS = 4
+BLOCKS_PER_DOT = 4
+MESH = pl.DeviceIdType.MESH
+
+
+def head_kernel(n_dp, n_cls, feat_ref, weight_ref, side_ref, rows_ref, coef_ref,
+                feats, wcols, exps, coefs, sides, lanes, labels, stats, all_stats, maxima, energies, scales,
+                send_sem, sib_send_sem, recv_sem, sib_recv_sem, wsend_sem, wrecv_sem,
+                ssend_sem, srecv_sem, tsend_sem, trecv_sem, local_sem, rows_sem, coef_sem):
+    me = lax.axis_index("dp")
+    cls = lax.axis_index("cls")
+    core = cls % 2
+    sibling = cls + 1 - 2 * core
+    stages = n_dp.bit_length() - 1
+    rows, depth = feat_ref.shape
+    half = rows // 2
+    chunks, _, depth_block, width = wcols.shape
+    cols = chunks * width
+    padded = lanes.shape[1]
+    row_block = rows_ref.shape[2]
+    per = BLOCKS_PER_DOT
+    count = CSPLIT * n_cls
+    place = me % CSPLIT * n_cls + cls
+
+    def group_peer(hop):
+        spot = (place + hop) % count
+        return (me // CSPLIT * CSPLIT + spot // n_cls, spot % n_cls)
+
+    barrier = pltpu.get_barrier_semaphore()
+    for hop in range(1, n_dp):
+        pl.semaphore_signal(barrier, inc=1, device_id=((me + hop) % n_dp, cls), device_id_type=MESH)
+    for hop in range(1, count):
+        pl.semaphore_signal(barrier, inc=1, device_id=group_peer(hop), device_id_type=MESH)
+    pl.semaphore_wait(barrier, n_dp - 1 + count - 1)
+
+    bit_step = [(1 << b) * (1 - 2 * ((me // (1 << b)) % 2)) for b in range(stages)]
+
+    def stage_steps(which):
+        table = [bit_step[b] for b in range(stages - 1, 1, -1)]
+        return table + [bit_step[1] * (1 - which) + bit_step[0] * which,
+                        bit_step[0] * (1 - which) + bit_step[1] * which]
+
+    steps = stage_steps(core)
+    sib_steps = stage_steps(1 - core)
+
+    def origin(mask, table):
+        spot = me
+        for s in range(stages):
+            if mask >> s & 1:
+                spot = spot + table[s]
+        return spot
+
+    mine = pl.ds(pl.multiple_of(core * half, half), half)
+    other = pl.ds(pl.multiple_of((1 - core) * half, half), half)
+    sends = []
+
+    def push(source, target, out_sem, in_sem, device):
+        copy = pltpu.make_async_remote_copy(
+            src_ref=source, dst_ref=target, send_sem=out_sem, recv_sem=in_sem,
+            device_id=device, device_id_type=MESH,
+        )
+        copy.start()
+        sends.append(copy)
+
+    def arrived(ref, sem):
+        pltpu.make_async_remote_copy(
+            src_ref=ref, dst_ref=ref, send_sem=sem, recv_sem=sem,
+            device_id=(me, sibling), device_id_type=MESH,
+        ).wait_recv()
+
+    def forward(mask, source, slot):
+        for s in range(mask.bit_length(), stages):
+            push(source, feats.at[slot, mine], send_sem.at[mask * stages + s],
+                 recv_sem.at[mask | 1 << s], (me + steps[s], cls))
+        if mask:
+            push(source, feats.at[slot, mine], sib_send_sem.at[mask], sib_recv_sem.at[mask], (me, sibling))
+
+    def send_chunk(c):
+        for hop in range(1, n_dp):
+            peer = (me + hop) % n_dp
+            first = pl.multiple_of(peer % CSPLIT * cols + c * width, width)
+            push(weight_ref.at[:, pl.ds(first, width)], wcols.at[c, me],
+                 wsend_sem.at[c * n_dp + hop], wrecv_sem.at[c * n_dp + hop], (peer, cls))
+
+    forward(0, feat_ref.at[mine], me)
+    keep = [
+        pltpu.make_async_copy(feat_ref, feats.at[me], local_sem.at[0]),
+        pltpu.make_async_copy(side_ref, sides.at[me], local_sem.at[1]),
+    ] + [
+        pltpu.make_async_copy(
+            weight_ref.at[:, pl.ds(pl.multiple_of(me % CSPLIT * cols + c * width, width), width)],
+            wcols.at[c, me], local_sem.at[2 + c])
+        for c in range(chunks)
+    ]
+    for copy in keep:
+        copy.start()
+    for hop in range(1, n_dp):
+        push(side_ref, sides.at[me], ssend_sem.at[hop], srecv_sem.at[hop], ((me + hop) % n_dp, cls))
+    for c in range(chunks):
+        send_chunk(c)
+
+    for hop in range(1, n_dp):
+        arrived(sides.at[(me + n_dp - hop) % n_dp], srecv_sem.at[hop])
+    for copy in keep:
+        copy.wait()
+    fill = jnp.zeros((128 - sides.shape[1], padded), jnp.float32)
+    lanes[...] = jnp.zeros_like(lanes)
+
+    def spread_labels(i, carry):
+        labels[i] = jnp.concatenate([sides[i], fill], axis=0).T
+        return carry
+
+    lax.fori_loop(0, n_dp, spread_labels, 0)
+    for i in range(n_dp):
+        energies[i:i + 1, :] = sides[i, 1:2, :]
+
+    for mask in range(1, n_dp):
+        slot = origin(mask, steps)
+        arrived(feats.at[slot, mine], recv_sem.at[mask])
+        forward(mask, feats.at[slot, mine], slot)
+    for mask in range(1, n_dp):
+        arrived(feats.at[origin(mask, sib_steps), other], sib_recv_sem.at[mask])
+
+    first_row = pl.multiple_of(me // CSPLIT * row_block, row_block)
+    row_copies = [
+        pltpu.make_async_copy(feats.at[i, :, pl.ds(first_row, row_block)], rows_ref.at[i], rows_sem.at[i])
+        for i in range(n_dp)
+    ]
+    for copy in row_copies:
+        copy.start()
+
+    base = cls * (CSPLIT * cols) + me % CSPLIT * cols
+
+    def hits(block_labels, c, shape):
+        offset = block_labels.astype(jnp.int32) - (base + c * width)
+        return lax.broadcasted_iota(jnp.int32, shape, 1) == offset
+
+    def chunk_body(c, carry):
+        for hop in range(1, n_dp):
+            arrived(wcols.at[c, (me + n_dp - hop) % n_dp], wrecv_sem.at[c * n_dp + hop])
+
+        def group_body(g, inner):
+            blocks = pl.ds(g * per, per)
+            logits = jnp.dot(
+                feats[blocks].reshape(per * rows, depth), wcols[c].reshape(depth, width),
+                preferred_element_type=jnp.float32)
+            hit = hits(labels[blocks, 0:rows, 0:1].reshape(per * rows, 1), c, logits.shape)
+            top = jnp.max(logits, axis=1, keepdims=True)
+            exponent = jnp.exp(logits - top)
+            total = jnp.sum(exponent, axis=1, keepdims=True)
+            square = jnp.sum(exponent * exponent, axis=1, keepdims=True)
+            picked = jnp.sum(jnp.where(hit, logits, 0.0), axis=1, keepdims=True)
+            exps[c, blocks] = exponent.reshape(per, rows, width)
+            held = lanes[blocks, 0:rows, :].reshape(per * rows, 128)
+            lane = lax.broadcasted_iota(jnp.int32, held.shape, 1) - 4 * c
+            held = jnp.where(lane == 0, top, held)
+            held = jnp.where(lane == 1, total, held)
+            held = jnp.where(lane == 2, square, held)
+            held = jnp.where(lane == 3, picked, held)
+            lanes[blocks, 0:rows, :] = held.reshape(per, rows, 128)
+            return inner
+
+        return lax.fori_loop(0, n_dp // per, group_body, carry)
+
+    lax.fori_loop(0, chunks, chunk_body, 0)
+
+    for i in range(n_dp):
+        turned = lanes[i].T
+        tops = [turned[4 * c:4 * c + 1] for c in range(chunks)]
+        top = functools.reduce(jnp.maximum, tops)
+        fades = [jnp.exp(t - top) for t in tops]
+        stats[0, i:i + 1, :] = top
+        stats[1, i:i + 1, :] = sum(turned[4 * c + 1:4 * c + 2] * fades[c] for c in range(chunks))
+        stats[2, i:i + 1, :] = sum(turned[4 * c + 2:4 * c + 3] * fades[c] * fades[c] for c in range(chunks))
+        stats[3, i:i + 1, :] = sum(turned[4 * c + 3:4 * c + 4] for c in range(chunks))
+        for c in range(chunks):
+            maxima[c, i:i + 1, :] = tops[c]
+
+    for hop in range(1, count):
+        push(stats, all_stats.at[place], tsend_sem.at[hop], trecv_sem.at[hop], group_peer(hop))
+    all_stats[pl.ds(place, 1)] = stats[...][None]
+    for hop in range(1, count):
+        arrived(all_stats.at[(place + count - hop) % count], trecv_sem.at[hop])
+
+    row_max = all_stats[0, 0]
+    for d in range(1, count):
+        row_max = jnp.maximum(row_max, all_stats[d, 0])
+    row_total = jnp.zeros_like(row_max)
+    row_square = jnp.zeros_like(row_max)
+    picked = jnp.zeros_like(row_max)
+    for d in range(count):
+        fade = jnp.exp(all_stats[d, 0] - row_max)
+        row_total = row_total + all_stats[d, 1] * fade
+        row_square = row_square + all_stats[d, 2] * fade * fade
+        picked = picked + all_stats[d, 3]
+    spread = row_square / (row_total * row_total) - 2.0 * jnp.exp(picked - row_max) / row_total + 1.0
+    factor = CLIP_NORM * lax.rsqrt(jnp.maximum(energies[...] * spread, CLIP_NORM * CLIP_NORM))
+    scales[chunks] = factor
+    for c in range(chunks):
+        scales[c] = factor * (jnp.exp(maxima[c] - row_max) / row_total)
+    for i in range(n_dp):
+        for c in range(chunks + 1):
+            sides[i, c:c + 1, :] = scales[c, i:i + 1, :]
+
+    def coef_copy(i):
+        return pltpu.make_async_copy(coefs.at[i], coef_ref.at[i], coef_sem.at[i])
+
+    def coef_body(i, carry):
+        columns = jnp.concatenate([sides[i], fill], axis=0).T[0:rows]
+        block_labels = labels[i, 0:rows, 0:1]
+        for c in range(chunks):
+            hit = hits(block_labels, c, (rows, width))
+            value = exps[c, i] * columns[:, c:c + 1] - jnp.where(hit, columns[:, chunks:chunks + 1], 0.0)
+            coefs[i, :, c * width:(c + 1) * width] = value.astype(coefs.dtype)
+        coef_copy(i).start()
+        return carry
+
+    lax.fori_loop(0, n_dp, coef_body, 0)
+    for i in range(n_dp):
+        coef_copy(i).wait()
+        row_copies[i].wait()
+    for copy in sends:
+        copy.wait_send()
+
+
+def head(features, weight, side, n_dp, n_cls, row_block, col_block):
+    stages = n_dp.bit_length() - 1
+    rows, depth = features.shape
+    padded = side.shape[1]
+    count = CSPLIT * n_cls
+    width = col_block // CHUNKS
+    anywhere = pl.BlockSpec(memory_space=pl.ANY)
+    dma = pltpu.SemaphoreType.DMA
+    f32 = jnp.float32
+    return pl.pallas_call(
+        functools.partial(head_kernel, n_dp, n_cls),
+        out_shape=(
+            jax.ShapeDtypeStruct((n_dp, rows, row_block), features.dtype),
+            jax.ShapeDtypeStruct((n_dp, rows, col_block), jnp.bfloat16),
+        ),
+        in_specs=[anywhere] * 3,
+        out_specs=(anywhere,) * 2,
+        scratch_shapes=[
+            pltpu.VMEM((n_dp, rows, depth), features.dtype),
+            pltpu.VMEM((CHUNKS, n_dp, weight.shape[0], width), weight.dtype),
+            pltpu.VMEM((CHUNKS, n_dp, rows, width), f32),
+            pltpu.VMEM((n_dp, rows, col_block), jnp.bfloat16),
+            pltpu.VMEM((n_dp,) + side.shape, f32),
+            pltpu.VMEM((n_dp, padded, 128), f32),
+            pltpu.VMEM((n_dp, padded, 128), f32),
+            pltpu.VMEM((4, n_dp, padded), f32),
+            pltpu.VMEM((count, 4, n_dp, padded), f32),
+            pltpu.VMEM((CHUNKS, n_dp, padded), f32),
+            pltpu.VMEM((n_dp, padded), f32),
+            pltpu.VMEM((CHUNKS + 1, n_dp, padded), f32),
+            dma((n_dp * stages,)), dma((n_dp,)), dma((n_dp,)), dma((n_dp,)),
+            dma((CHUNKS * n_dp,)), dma((CHUNKS * n_dp,)),
+            dma((n_dp,)), dma((n_dp,)), dma((count,)), dma((count,)),
+            dma((2 + CHUNKS,)), dma((n_dp,)), dma((n_dp,)),
+        ],
+        compiler_params=pltpu.CompilerParams(
+            collective_id=0, has_side_effects=True, vmem_limit_bytes=60 << 20),
+    )(features, weight, side)
+
+
+def examples_split(features, labels, weight, noise):
     tok_rows = features.shape[0]
     feature_dim = features.shape[1]
     class_shard = weight.shape[1]
@@ -58,6 +324,24 @@
     return (grad_block + NOISE_STD * noise[0, 0]).reshape(noise.shape)
 
 
+def on_device(features, labels, weight, noise):
+    n_dp = lax.axis_size("dp")
+    if n_dp * features.size * features.dtype.itemsize > GATHER_LIMIT:
+        return examples_split(features, labels, weight, noise)
+    feature_dim = features.shape[1]
+    class_shard = weight.shape[1]
+    groups = n_dp // CSPLIT
+    row_block = feature_dim // groups
+    col_block = class_shard // CSPLIT
+    padded = -(-features.shape[0] // 128) * 128
+    own_energy = jnp.sum(jnp.square(features.astype(jnp.float32)), axis=1)
+    side = jnp.pad(
+        jnp.stack([labels.astype(jnp.float32), own_energy]), ((0, 6), (0, padded - features.shape[0])))
+    rows, coef = head(features, weight, side, n_dp, lax.axis_size("cls"), row_block, col_block)
+    grad = lax.dot_general(rows, coef, (((0, 1), (0, 1)), ((), ())), preferred_element_type=jnp.float32)
+    return (grad + NOISE_STD * noise[0, 0]).reshape(noise.shape)
+
+
 def solution(mesh):
     placed = (P("dp", None), P("dp"), P("dp", "cls"), P("dp", "cls", None, None))
     return jax.shard_map(

time: 692 us -> 195 us (0.28)
  the two profiles are of different devices: /device:TPU:28 before, /device:TPU:7 now
where the time goes in v3:
time: 195 us
  Pallas kernels  180 us (92%)
  matrix products  12.6 us (6%)
  other arithmetic  2.66 us (1%)
    pallas_call x1, Pallas kernels, head(): pl.pallas_call(functools.partial(head_kernel, n_dp, n_cls), out_shape=(ja...  180 us
    dot_general x1, matrix products, on_device(): lax.dot_general(rows, coef, (((0, 1), (0, 1)), ((), ())), preferred_eleme...  12.6 us

profile of v3, /device:TPU:7, one launch (start us, length us, event | category | flops | bytes accessed | tf_op | source)
XLA Modules:
  0.0 194.9 jit_solution(6486855832184773473)
XLA Ops:
  0.0 0.7 convert_element_type.8
  0.7 1.4 multiply_reduce_fusion
  2.1 0.6 select_maximum_fusion.side_ref
  2.7 179.6 %shard_map.46 = (bf16[16,192,1024]{2,1,0:T(8,128)(2,1)}, bf16[16,192,1024]{2,1,0:T(8,128)(2,1)}) custom-call(bf16[192,2048]{1,0:T(8,128)(2,1)} %feat_ref.1, bf16[128,8192]{1,0:T(8,128)(2,1)} %weight_ref.1, f32[8,256]{1,0:T(8,128)} %select_maximum_fusion.side_ref), custom_call_target="tpu_custom_call" | custom-call | tf_op jit(solution)/shard_map/pallas_call | solution.py:248
  182.3 12.6 %fusion = f32[1,1,1024,1024]{3,2,1,0:T(8,128)} fusion(f32[1,1,1024,1024]{3,2,1,0:T(8,128)} %param.7, bf16[16,192,1024]{2,1,0:T(8,128)(2,1)} %get-tuple-element.7, bf16[16,192,1024]{2,1,0:T(8,128)(2,1)} %get-tuple-element.8), kind=kOutput, calls=%fused_computation.1 | convolution fusion | flops 6444548096 | bytes 20971520 | tf_op jit(solution)/shard_map/dot_general | solution.py:341

commit v4 on v3

--- a/solution.py
+++ b/solution.py
@@ -12,7 +12,7 @@
 NOISE_STD = 0.4
 GATHER_LIMIT = 16 << 20
 CHUNKS = 4
-BLOCKS_PER_DOT = 4
+BLOCKS_PER_DOT = 8
 MESH = pl.DeviceIdType.MESH
 
 
@@ -109,8 +109,6 @@
         copy.start()
     for hop in range(1, n_dp):
         push(side_ref, sides.at[me], ssend_sem.at[hop], srecv_sem.at[hop], ((me + hop) % n_dp, cls))
-    for c in range(chunks):
-        send_chunk(c)
 
     for hop in range(1, n_dp):
         arrived(sides.at[(me + n_dp - hop) % n_dp], srecv_sem.at[hop])
@@ -131,6 +129,8 @@
         slot = origin(mask, steps)
         arrived(feats.at[slot, mine], recv_sem.at[mask])
         forward(mask, feats.at[slot, mine], slot)
+        if mask % (n_dp // chunks) == 1:
+            send_chunk(mask // (n_dp // chunks))
     for mask in range(1, n_dp):
         arrived(feats.at[origin(mask, sib_steps), other], sib_recv_sem.at[mask])
 

time: 195 us -> 175 us (0.90)
  Pallas kernels: 180 us -> 160 us
    pallas_call x1, Pallas kernels: 180 us -> 160 us  [head(): pl.pallas_call(functools.partial(head_kernel, n_dp, n_cls), out_shape=(ja...]
where the time goes in v4:
time: 175 us
  Pallas kernels  160 us (91%)
  matrix products  12.6 us (7%)
  other arithmetic  2.66 us (2%)
    pallas_call x1, Pallas kernels, head(): pl.pallas_call(functools.partial(head_kernel, n_dp, n_cls), out_shape=(ja...  160 us
    dot_general x1, matrix products, on_device(): lax.dot_general(rows, coef, (((0, 1), (0, 1)), ((), ())), preferred_eleme...  12.6 us

profile of v4, /device:TPU:7, one launch (start us, length us, event | category | flops | bytes accessed | tf_op | source)
XLA Modules:
  0.0 175.3 jit_solution(3959576119336630748)
XLA Ops:
  0.0 0.7 convert_element_type.8
  0.7 1.4 multiply_reduce_fusion
  2.1 0.6 select_maximum_fusion.side_ref
  2.7 160.0 %shard_map.46 = (bf16[16,192,1024]{2,1,0:T(8,128)(2,1)}, bf16[16,192,1024]{2,1,0:T(8,128)(2,1)}) custom-call(bf16[192,2048]{1,0:T(8,128)(2,1)} %feat_ref.1, bf16[128,8192]{1,0:T(8,128)(2,1)} %weight_ref.1, f32[8,256]{1,0:T(8,128)} %select_maximum_fusion.side_ref), custom_call_target="tpu_custom_call" | custom-call | tf_op jit(solution)/shard_map/pallas_call | solution.py:248
  162.6 12.6 %fusion = f32[1,1,1024,1024]{3,2,1,0:T(8,128)} fusion(f32[1,1,1024,1024]{3,2,1,0:T(8,128)} %param.7, bf16[16,192,1024]{2,1,0:T(8,128)(2,1)} %get-tuple-element.7, bf16[16,192,1024]{2,1,0:T(8,128)(2,1)} %get-tuple-element.8), kind=kOutput, calls=%fused_computation.1 | convolution fusion | flops 6444548096 | bytes 20971520 | tf_op jit(solution)/shard_map/dot_general | solution.py:341
